TPU v7x, 128 devices: a whole 4x4x4 slice. The times are simulated.
128 devices in a mesh: net: 8 (over z, core), strip: 16 (over y, x).
Axes of the slice: x: 4, y: 4, z: 4, core: 2. Of those that a mesh axis runs over, the one named last changes fastest.
Arguments:
- cond_charge: bfloat16 [3072, 32, 128], P(('net', 'strip')), may hold values from -6 to 6
- cond_live: int32 [128], P(('net', 'strip')), may hold values from 2 to 24, as said below
- near_src: int32 [3072, 16], P(('net', 'strip')), may hold values from -1 to 3071, as said below
- near_mat: bfloat16 [3072, 16, 128, 128], P(('net', 'strip')), may hold values from -0.125 to 0.125
- cond_basis: bfloat16 [3072, 16, 128], P(('net', 'strip')), may hold values from -0.5 to 0.5
- cond_rank: int32 [3072], P(('net', 'strip')), may hold values from 8 to 16
- far_src: int32 [3072, 16], P(('net', 'strip')), may hold values from -1 to 3583, as said below
- far_mat: bfloat16 [3072, 16, 16, 16], P(('net', 'strip')), may hold values from -0.375 to 0.375
- iface_charge: bfloat16 [512, 32, 128], P('strip', 'net'), may hold values from -6 to 6
- iface_near: bfloat16 [512, 3, 128, 128], P('strip'), may hold values from -0.3125 to 0.3125
- iface_basis: bfloat16 [512, 16, 128], P('strip'), may hold values from -0.5 to 0.5
- iface_rank: int32 [512], P('strip'), may hold values from 8 to 16
- iface_far_src: int32 [512, 16], P('strip'), may hold values from -1 to 3583, as said below
- iface_far_mat: bfloat16 [512, 16, 16, 16], P('strip'), may hold values from -0.375 to 0.375
Outputs:
- cond_pot: bfloat16 [3072, 32, 128], P(('net', 'strip'))
- iface_pot: bfloat16 [512, 32, 128], P('strip', 'net')
Inputs may be any that keep to these rules, and one draw needn't show every extreme that they name: `cond_live`: in every draw, two devices of every net group have all 24 slots live; live slots are the first ones of a device. `near_src`: entry 0 of a row is the row's own block. Every other entry is -1 (padding, only after the used entries) or a live conductor slot of a device with the same net index as the row's device. `far_src`: each entry is -1 (padding, only after the used entries), a live conductor slot, or an interface block number. `iface_far_src`: each entry is -1 (padding, only after the used entries), a live conductor slot, or an interface block number.
All inputs are finite; a program needn't handle non-finite values.
Results may differ from a plain program's by a relative error of at most 0.0027.
Values may be sent and summed in bfloat16 or wider, within the bound.
No kernel may reach another device: no remote copies, remote signals or barrier semaphores. Data moves between devices by JAX's collectives and lax.ppermute only.
A program may use at most 128 MiB of HBM per device.

v0:
```python
import jax
import jax.numpy as jnp
from jax import lax
from jax.sharding import PartitionSpec as P


def extended(array, sides, width):
    for axis, dim in sides:
        peers, length = (lax.axis_size(axis), array.shape[dim])
        up = [(i, (i + 1) % peers) for i in range(peers - 1)]
        down = [(j, i) for i, j in up]
        last = lax.slice_in_dim(array, length - width, length, axis=dim)
        leading = lax.slice_in_dim(array, 0, width, axis=dim)
        before = lax.ppermute(last, axis, up)
        after = lax.ppermute(leading, axis, down)
        array = jnp.concatenate([before, array, after], axis=dim)
    return array


def coeffs(block_basis, charge, block_rank):
    product = jnp.einsum("tap,trp->tar", block_basis, charge, preferred_element_type=jnp.float32)
    keep_rows = (jnp.arange(block_basis.shape[1])[None, :] < block_rank[:, None]).astype(
        jnp.float32
    )
    return (product * keep_rows[:, :, None]).astype(jnp.bfloat16)


def far_field(source_ids, far_mats, block_basis, block_rank, coef_table):
    usable = (source_ids >= 0).astype(jnp.bfloat16)
    fetched = coef_table[jnp.maximum(source_ids, 0)] * usable[:, :, None, None]
    gathered_far = jnp.einsum(
        "tkab,tkbr->tar", far_mats, fetched, preferred_element_type=jnp.float32
    )
    keep_rows = (jnp.arange(block_basis.shape[1])[None, :] < block_rank[:, None]).astype(
        jnp.float32
    )
    gathered_far = (gathered_far * keep_rows[:, :, None]).astype(jnp.bfloat16)
    return jnp.einsum("tap,tar->trp", block_basis, gathered_far, preferred_element_type=jnp.float32)


def shards(
    cond_charge,
    cond_live,
    near_src,
    near_mat,
    cond_basis,
    cond_rank,
    far_src,
    far_mat,
    iface_charge,
    iface_near,
    iface_basis,
    iface_rank,
    iface_far_src,
    iface_far_mat,
):
    cond_blocks = cond_charge.shape[0]
    iface_blocks = iface_charge.shape[0]
    excite_rows = iface_charge.shape[1]
    strip_count = lax.axis_size("strip")
    net_index = lax.axis_index("net")
    grouped = lax.all_gather(cond_charge, "strip", axis=0, tiled=True)
    local_ids = near_src - net_index * strip_count * cond_blocks
    usable = (near_src >= 0).astype(jnp.bfloat16)
    fetched = grouped[jnp.clip(local_ids, 0, grouped.shape[0] - 1)] * usable[:, :, None, None]
    near_part = jnp.einsum("tkpq,tkrq->trp", near_mat, fetched, preferred_element_type=jnp.float32)
    rimmed = extended(iface_charge, (("strip", 0),), 1)
    iface_near_part = jnp.einsum(
        "tpq,trq->trp", iface_near[:, 0], rimmed[:iface_blocks], preferred_element_type=jnp.float32
    )
    iface_near_part = iface_near_part + jnp.einsum(
        "tpq,trq->trp",
        iface_near[:, 1],
        rimmed[1 : iface_blocks + 1],
        preferred_element_type=jnp.float32,
    )
    iface_near_part = iface_near_part + jnp.einsum(
        "tpq,trq->trp", iface_near[:, 2], rimmed[2:], preferred_element_type=jnp.float32
    )
    cond_coef = coeffs(cond_basis, cond_charge, cond_rank)
    iface_local = coeffs(iface_basis, iface_charge, iface_rank)
    iface_full = lax.all_gather(iface_local, "net", axis=2, tiled=True)
    cond_table = lax.all_gather(cond_coef, ("net", "strip"), axis=0, tiled=True)
    iface_table = lax.all_gather(iface_full, "strip", axis=0, tiled=True)
    coef_table = jnp.concatenate([cond_table, iface_table], 0)
    cond_far = far_field(far_src, far_mat, cond_basis, cond_rank, coef_table)
    excite_table = lax.dynamic_slice_in_dim(coef_table, net_index * excite_rows, excite_rows, 2)
    iface_far = far_field(iface_far_src, iface_far_mat, iface_basis, iface_rank, excite_table)
    alive_mask = (jnp.arange(cond_blocks) < cond_live[0]).astype(jnp.float32)
    cond_pot = ((near_part + cond_far) * alive_mask[:, None, None]).astype(jnp.bfloat16)
    iface_pot = (iface_near_part + iface_far).astype(jnp.bfloat16)
    return (cond_pot, iface_pot)


def solution(mesh):
    placed = (
        P(("net", "strip"), None, None),
        P(("net", "strip")),
        P(("net", "strip"), None),
        P(("net", "strip"), None, None, None),
        P(("net", "strip"), None, None),
        P(("net", "strip")),
        P(("net", "strip"), None),
        P(("net", "strip"), None, None, None),
        P("strip", "net", None),
        P("strip", None, None, None),
        P("strip", None, None),
        P("strip"),
        P("strip", None),
        P("strip", None, None, None),
    )
    return jax.shard_map(
        shards,
        mesh=mesh,
        in_specs=placed,
        out_specs=(P(("net", "strip"), None, None), P("strip", "net", None)),
        check_vma=False,
    )
```

profile of v0, /device:TPU:1, one launch (start us, length us, event | category | flops | bytes accessed | tf_op | source)
XLA Modules:
  0.0 214.6 jit_solution(11559196575613654127)
XLA Ops:
  7.2 0.0 copy-start
  7.2 0.0 copy-start.7
  7.2 0.0 copy-start.10
  7.2 0.0 all-gather.3.cloned.1.call-start
  7.3 0.7 all-gather.3.cloned.1.call-update
  8.0 0.0 all-gather.5.cloned.1.call-start
  8.0 0.7 fusion.50
  8.7 1.8 fusion.19
  10.6 0.0 all-gather.5.cloned.1.call-update
  10.6 0.7 fusion.53
  11.3 1.3 collective-permute-start.1
  12.6 4.6 %collective-permute-start = (bf16[1,4,128]{2,1,0:T(4,128)(2,1)S(1)}, bf16[1,4,128]{2,1,0:T(4,128)(2,1)S(1)}, u32[]{:S(2)}, u32[]{:S(2)}) collective-permute-start(bf16[1,4,128]{2,1,0:T(4,128)(2,1)S(1)} %get-tuple-element.2), channel_id=1, source_target_pairs={{0,1},{1,2},{2,3},{3,4},{4,5},{5,6},{6,7},{7,8},{8,9},{9,10},{10,1... | collective-permute-start | bytes 3080 | tf_op jit(solution)/shard_map/ppermute | solution.py:14
  17.2 0.7 fusion.49
  17.9 0.9 fusion.27
  18.8 0.1 copy.71
  18.9 15.3 %all_gather.14 = bf16[32,16,32]{0,1,2:T(8,128)(2,1)S(1)} all-gather(bf16[32,16,4]{0,1,2:T(8,128)(2,1)S(1)} %copy.71), channel_id=1, replica_groups=mesh['net'=8,'strip'=16] {'net'}, dimensions={2}, use_global_device_ids=true | all-gather | bytes 36864 | tf_op jit(solution)/shard_map/all_gather | solution.py:82
  34.2 0.2 copy.72
  34.4 0.7 broadcast_maximum_fusion
  35.1 0.1 copy.79
  35.2 0.1 reshape.74
  35.3 0.7 broadcast_maximum_fusion.1
  36.0 0.1 copy.73
  36.0 0.1 reshape.66
  36.1 0.7 compare_select_fusion
  36.8 0.1 copy.69
  36.9 0.1 reshape.58
  37.7 32.7 %all_gather.15 = bf16[512,16,32]{2,1,0:T(8,128)(2,1)} all-gather(bf16[32,16,32]{2,1,0:T(8,128)(2,1)S(1)} %copy.72), channel_id=1, replica_groups=mesh['net'=8,'strip'=16] {'strip'}, dimensions={0}, use_global_device_ids=true | all-gather | bytes 557056 | tf_op jit(solution)/shard_map/all_gather | solution.py:84
  70.5 1.9 fusion.31
  72.3 0.1 copy.82
  72.4 4.4 %copy.84 = bf16[32,16,16,16]{2,1,3,0:T(8,128)(2,1)} copy(bf16[32,16,16,16]{0,3,2,1:T(8,128)(2,1)S(1)} %copy-done.4) | data formatting | bytes 524288 | tf_op args[13]
  76.8 0.1 copy.70
  76.9 3.5 %copy.75 = bf16[24,16,16,16]{3,2,1,0:T(8,128)(2,1)} copy(bf16[24,16,16,16]{0,3,2,1:T(8,128)(2,1)S(1)} %copy-done.5) | data formatting | bytes 393216 | tf_op args[7]
  80.3 0.1 copy.74
  80.4 1.9 fusion.29
  82.3 3.2 %gather_fusion = bf16[384,32,128]{2,1,0:T(8,128)(2,1)S(1)} fusion(bf16[384,32,128]{2,1,0:T(8,128)(2,1)} %all-gather.3.cloned.1.call-done, s32[1024]{0:T(1024)S(1)} %pad_clamp_fusion.2), kind=kCustom, calls=%fused_computation | custom fusion | bytes 6292992 | tf_op jit(solution)/shard_map/gather | solution.py:65
  85.5 8.0 %fusion.6 = f32[24,32,128]{2,1,0:T(8,128)} fusion(bf16[24,16,128,128]{3,2,1,0:T(8,128)(2,1)} %param.17, bf16[24,16,32,128]{3,2,1,0:T(8,128)(2,1)S(1)} %bitcast.52, bf16[24,16]{1,0:T(8,128)(2,1)S(1)} %copy.70), kind=kOutput, calls=%fused_computation.10 | convolution fusion | flops 404226048 | bytes 16122624 | tf_op jit(solution)/shard_map/tkpq,tkrq->trp/dot_general | solution.py:66
  93.5 50.7 %all-gather.5.cloned.1.call-done = bf16[3072,16,32]{2,1,0:T(8,128)(2,1)} async-done(((bf16[24,16,32]{2,1,0:T(8,128)(2,1)}), bf16[3072,16,32]{2,1,0:T(8,128)(2,1)}) %all-gather.5.cloned.1.call-update) | async-done | bytes 3145744 | tf_op jit(solution)/shard_map/all_gather | solution.py:83
  144.2 6.8 %constant_dynamic-update-slice_fusion.1 = bf16[3584,16,32]{2,1,0:T(8,128)(2,1)S(1)} fusion(bf16[3072,16,32]{2,1,0:T(8,128)(2,1)} %all-gather.5.cloned.1.call-done), kind=kLoop, calls=%fused_computation.58 | loop fusion | bytes 15728640
  151.0 0.5 constant_dynamic-update-slice_fusion
  151.6 5.2 %copy-done.1 = bf16[3584,16,32]{2,1,0:T(8,128)(2,1)} copy-done((bf16[3584,16,32]{2,1,0:T(8,128)(2,1)}, bf16[3584,16,32]{2,1,0:T(8,128)(2,1)S(1)}, u32[]{:S(2)}) %copy-start.1) | copy-done | bytes 3670040
  156.8 7.8 %constant_dynamic-slice_fusion = bf16[3584,16,4]{2,1,0:T(8,128)(2,1)} fusion(bf16[3584,16,32]{2,1,0:T(8,128)(2,1)S(1)} %constant_dynamic-update-slice_fusion, s32[]{:T(128)S(6)} %select_n.9), kind=kLoop, calls=%fused_computation.62 | loop fusion | bytes 917508 | tf_op jit(solution)/shard_map/dynamic_slice | solution.py:87
  164.6 24.0 %copy.80 = bf16[3584,16,4]{1,2,0:T(4,128)(2,1)} copy(bf16[3584,16,4]{2,1,0:T(8,128)(2,1)} %constant_dynamic-slice_fusion) | data formatting | bytes 917504 | tf_op jit(solution)/shard_map/dynamic_slice | solution.py:87
  188.6 3.5 %gather_fusion.2 = bf16[512,16,4]{1,2,0:T(4,128)(2,1)S(1)} fusion(bf16[3584,16,4]{1,2,0:T(4,128)(2,1)} %copy.80, s32[1024]{0:T(1024)S(1)} %pad_clamp_fusion), kind=kCustom, calls=%fused_computation.2 | custom fusion | bytes 133120 | tf_op jit(solution)/shard_map/gather | solution.py:30
  192.2 0.9 copy.88
  193.1 7.2 %gather_fusion.1 = bf16[384,16,32]{2,1,0:T(8,128)(2,1)} fusion(bf16[3584,16,32]{2,1,0:T(8,128)(2,1)} %copy-done.1, s32[1024]{0:T(1024)S(1)} %pad_clamp_fusion.1), kind=kCustom, calls=%fused_computation.1 | custom fusion | bytes 787968 | tf_op jit(solution)/shard_map/gather | solution.py:30
  200.4 3.9 %fusion.9 = bf16[24,32,128]{2,1,0:T(8,128)(2,1)} fusion(f32[24,32,128]{2,1,0:T(8,128)S(1)} %copy-done.6, bf16[24,16,128]{2,1,0:T(8,128)(2,1)S(1)} %copy-done.8, bf16[24,16,16,16]{3,2,1,0:T(8,128)(2,1)} %copy.75, bf16[24,16,16,32]{3,2,1,0:T(8,128)(2,1)} %bitcast.53, bf16[24,16]{1,0:T(8,128)(2,1)S(1)} %copy.74, f32[24]{0:T(128)S(1)} %compare_convert_fusion.3, ...), kind=kOutput, calls=%fused_computation.11 | convolution fusion | flops 10543104 | bytes 1280352 | tf_op jit(solution)/shard_map/tap,tar->trp/dot_general | solution.py:38
  204.3 0.9 fusion.28
  205.2 2.5 %fusion.25 = bf16[32,4,128]{2,1,0:T(4,128)(2,1)} fusion(f32[32,4,128]{2,1,0:T(4,128)S(1)} %fusion.28, f32[32,4,128]{2,1,0:T(4,128)S(1)} %fusion.29, f32[32,4,128]{2,1,0:T(4,128)S(1)} %fusion.31, bf16[32,3,128,128]{3,2,1,0:T(8,128)(2,1)} %param.23, bf16[32,4,128]{2,1,0:T(4,128)(2,1)S(1)} %copy-done.7, bf16[1,4,128]{2,1,0:T(4,128)(2,1)S(1)} %collective-permute-done), kind=kOutput, calls=%fused_computation.23 | convolution fusion | flops 4327424 | bytes 1311744 | tf_op jit(solution)/shard_map/tpq,trq->trp/dot_general | solution.py:68
  (31 shorter events, 0.1 us)
Async XLA Ops:
  7.2 10.7 %copy-start = (bf16[32,16,128]{2,1,0:T(8,128)(2,1)S(1)}, bf16[32,16,128]{2,1,0:T(8,128)(2,1)}, u32[]{:S(2)}) copy-start(bf16[32,16,128]{2,1,0:T(8,128)(2,1)} %param.24) | copy-start | bytes 393220
  7.2 63.3 %copy-start.7 = (bf16[32,4,128]{2,1,0:T(4,128)(2,1)S(1)}, bf16[32,4,128]{2,1,0:T(4,128)(2,1)}, u32[]{:S(2)}) copy-start(bf16[32,4,128]{2,1,0:T(4,128)(2,1)} %param.22) | copy-start | bytes 98308
  7.2 63.2 %copy-start.9 = (s32[32,16]{0,1:T(8,128)S(1)}, s32[32,16]{0,1:T(8,128)}, u32[]{:S(2)}) copy-start(s32[32,16]{0,1:T(8,128)} %param.26) | copy-start | bytes 6148
  7.2 63.2 %copy-start.11 = (s32[24,16]{0,1:T(8,128)S(1)}, s32[24,16]{0,1:T(8,128)}, u32[]{:S(2)}) copy-start(s32[24,16]{0,1:T(8,128)} %param.20) | copy-start | bytes 4612
  7.2 63.2 %copy-start.10 = (s32[24,16]{0,1:T(8,128)S(1)}, s32[24,16]{0,1:T(8,128)}, u32[]{:S(2)}) copy-start(s32[24,16]{0,1:T(8,128)} %param.16) | copy-start | bytes 4612
  7.2 65.2 %copy-start.4 = (bf16[32,16,16,16]{0,3,2,1:T(8,128)(2,1)S(1)}, bf16[32,16,16,16]{0,3,2,1:T(8,128)(2,1)}, u32[]{:S(2)}) copy-start(bf16[32,16,16,16]{0,3,2,1:T(8,128)(2,1)} %param.27) | copy-start | bytes 786436
  7.2 75.1 %all-gather.3.cloned.1.call-start = ((), (), s32[]{:S(2)}) async-start(), calls=%async_computation | async-start | bytes 3342336 | tf_op jit(solution)/shard_map/all_gather | solution.py:62
  8.0 136.2 %all-gather.5.cloned.1.call-start = ((), (), s32[]{:S(2)}) async-start(), calls=%async_computation.1 | async-start | bytes 12681216 | tf_op jit(solution)/shard_map/all_gather | solution.py:83
  11.3 69.1 %collective-permute-start.1 = (bf16[1,4,128]{2,1,0:T(4,128)(2,1)S(1)}, bf16[1,4,128]{2,1,0:T(4,128)(2,1)S(1)}, u32[]{:S(2)}, u32[]{:S(2)}) collective-permute-start(bf16[1,4,128]{2,1,0:T(4,128)(2,1)S(1)} %get-tuple-element.3), channel_id=1, source_target_pairs={{1,0},{2,1},{3,2},{4,3},{5,4},{6,5},{7,6},{8,7},{9,8},{10,9},{11,1... | collective-permute-start | bytes 3080 | tf_op jit(solution)/shard_map/ppermute | solution.py:15
  12.6 192.6 %collective-permute-start = (bf16[1,4,128]{2,1,0:T(4,128)(2,1)S(1)}, bf16[1,4,128]{2,1,0:T(4,128)(2,1)S(1)}, u32[]{:S(2)}, u32[]{:S(2)}) collective-permute-start(bf16[1,4,128]{2,1,0:T(4,128)(2,1)S(1)} %get-tuple-element.2), channel_id=1, source_target_pairs={{0,1},{1,2},{2,3},{3,4},{4,5},{5,6},{6,7},{7,8},{8,9},{9,10},{10,1... | collective-permute-start | bytes 3080 | tf_op jit(solution)/shard_map/ppermute | solution.py:14
  37.7 39.2 %copy-start.5 = (bf16[24,16,16,16]{0,3,2,1:T(8,128)(2,1)S(1)}, bf16[24,16,16,16]{0,3,2,1:T(8,128)(2,1)}, u32[]{:S(2)}) copy-start(bf16[24,16,16,16]{0,3,2,1:T(8,128)(2,1)} %param.21) | copy-start | bytes 589828
  93.5 57.6 %copy-start.2 = (bf16[512,16,32]{2,1,0:T(8,128)(2,1)S(1)}, bf16[512,16,32]{2,1,0:T(8,128)(2,1)}, u32[]{:S(2)}) copy-start(bf16[512,16,32]{2,1,0:T(8,128)(2,1)} %all_gather.15) | copy-start | bytes 1572868
  151.5 5.2 %copy-start.1 = (bf16[3584,16,32]{2,1,0:T(8,128)(2,1)}, bf16[3584,16,32]{2,1,0:T(8,128)(2,1)S(1)}, u32[]{:S(2)}) copy-start(bf16[3584,16,32]{2,1,0:T(8,128)(2,1)S(1)} %constant_dynamic-update-slice_fusion) | copy-start | bytes 11010052
  192.1 8.2 %copy-start.6 = (f32[24,32,128]{2,1,0:T(8,128)S(1)}, f32[24,32,128]{2,1,0:T(8,128)}, u32[]{:S(2)}) copy-start(f32[24,32,128]{2,1,0:T(8,128)} %fusion.6) | copy-start | bytes 1179652
  192.2 8.2 %copy-start.8 = (bf16[24,16,128]{2,1,0:T(8,128)(2,1)S(1)}, bf16[24,16,128]{2,1,0:T(8,128)(2,1)}, u32[]{:S(2)}) copy-start(bf16[24,16,128]{2,1,0:T(8,128)(2,1)} %param.18) | copy-start | bytes 294916
  200.4 4.0 %copy-start.3 = (bf16[32,16,16,16]{2,1,3,0:T(8,128)(2,1)S(1)}, bf16[32,16,16,16]{2,1,3,0:T(8,128)(2,1)}, u32[]{:S(2)}) copy-start(bf16[32,16,16,16]{2,1,3,0:T(8,128)(2,1)} %copy.84) | copy-start | bytes 786436
Sparse Core Ops, SparseCore 0:
  10.2 54.1 all-gather.2
  67.9 76.2 all-gather.4
where the time goes:
time: 215 us
  local copies, waits for them, and re-layouts  68.8 us (32%)
  waiting for transfers between devices  51.5 us (24%)
  blocking collectives  47.9 us (22%)
  matrix products  21.8 us (10%)
  between operations  15 us (7%)
  starting transfers between devices  5.92 us (3%)
  other arithmetic  3.64 us (2%)
    all_gather x1, waiting for transfers between devices, shards(): cond_table = lax.all_gather(cond_coef, ('net', 'strip'), axis=0, tiled=True)  50.7 us
    all_gather x1, blocking collectives, shards(): iface_table = lax.all_gather(iface_full, 'strip', axis=0, tiled=True)  32.7 us
    dynamic_slice x2, local copies, waits for them, and re-layouts, shards(): lax.dynamic_slice_in_dim(coef_table, net_index * excite_rows, excite_rows...  31.9 us
    unnamed x27, local copies, waits for them, and re-layouts  19.9 us
    all_gather x1, blocking collectives, shards(): iface_full = lax.all_gather(iface_local, 'net', axis=2, tiled=True)  15.3 us
    gather x3, local copies, waits for them, and re-layouts, far_field(): fetched = coef_table[jnp.maximum(source_ids, 0)] * usable[:, :, None, None]  11.7 us
    dot_general x1, matrix products, shards(): jnp.einsum('tkpq,tkrq->trp', near_mat, fetched, preferred_element_type=jn...  8.01 us
    dot_general x2, matrix products, far_field(): jnp.einsum('tap,tar->trp', block_basis, gathered_far, preferred_element_t...  4.8 us
  transfers between devices with their start and end apart: 4, of which 1 were waited for; matrix products, arithmetic and copies ran while one was open for 40% of the time, Pallas kernels for 0%

commit v1 on v0

--- a/solution.py
+++ b/solution.py
@@ -79,7 +79,7 @@
     )
     cond_coef = coeffs(cond_basis, cond_charge, cond_rank)
     iface_local = coeffs(iface_basis, iface_charge, iface_rank)
-    iface_full = lax.all_gather(iface_local, "net", axis=2, tiled=True)
+    iface_full = jnp.concatenate(lax.all_gather(iface_local, "net"), axis=2)
     cond_table = lax.all_gather(cond_coef, ("net", "strip"), axis=0, tiled=True)
     iface_table = lax.all_gather(iface_full, "strip", axis=0, tiled=True)
     coef_table = jnp.concatenate([cond_table, iface_table], 0)

time: 215 us -> 215 us (level)
  no operation moved by 1% of the time
where the time goes in v1:
time: 215 us; the launch traced here: 214 us
  local copies, waits for them, and re-layouts  68.9 us (32%)
  waiting for transfers between devices  51.1 us (24%)
  blocking collectives  48.1 us (22%)
  matrix products  21.8 us (10%)
  between operations  15 us (7%)
  starting transfers between devices  5.92 us (3%)
  other arithmetic  3.64 us (2%)
    all_gather x1, waiting for transfers between devices, shards(): cond_table = lax.all_gather(cond_coef, ('net', 'strip'), axis=0, tiled=True)  50.4 us
    all_gather x1, blocking collectives, shards(): iface_table = lax.all_gather(iface_full, 'strip', axis=0, tiled=True)  32.7 us
    dynamic_slice x2, local copies, waits for them, and re-layouts, shards(): lax.dynamic_slice_in_dim(coef_table, net_index * excite_rows, excite_rows...  31.9 us
    unnamed x27, local copies, waits for them, and re-layouts  19.9 us
    all_gather x1, blocking collectives, shards(): iface_full = jnp.concatenate(lax.all_gather(iface_local, 'net'), axis=2)  15.3 us
    gather x3, local copies, waits for them, and re-layouts, far_field(): fetched = coef_table[jnp.maximum(source_ids, 0)] * usable[:, :, None, None]  11.7 us
    dot_general x1, matrix products, shards(): jnp.einsum('tkpq,tkrq->trp', near_mat, fetched, preferred_element_type=jn...  8.02 us
    dot_general x2, matrix products, far_field(): jnp.einsum('tap,tar->trp', block_basis, gathered_far, preferred_element_t...  4.8 us
  transfers between devices with their start and end apart: 4, of which 1 were waited for; matrix products, arithmetic and copies ran while one was open for 40% of the time, Pallas kernels for 0%

profile of v1, /device:TPU:1, one launch (start us, length us, event | category | flops | bytes accessed | tf_op | source)
XLA Modules:
  0.0 214.5 jit_solution(8614310691610675653)
XLA Ops:
  7.2 0.0 copy-start
  7.2 0.0 copy-start.7
  7.2 0.0 copy-start.10
  7.2 0.0 all-gather.4.cloned.1.call-start
  7.3 0.7 all-gather.4.cloned.1.call-update
  8.0 0.0 all-gather.6.cloned.1.call-start
  8.0 0.7 fusion.50
  8.7 1.8 fusion.19
  10.6 0.0 all-gather.6.cloned.1.call-update
  10.6 0.7 fusion.53
  11.3 1.3 collective-permute-start.1
  12.6 4.6 %collective-permute-start = (bf16[1,4,128]{2,1,0:T(4,128)(2,1)S(1)}, bf16[1,4,128]{2,1,0:T(4,128)(2,1)S(1)}, u32[]{:S(2)}, u32[]{:S(2)}) collective-permute-start(bf16[1,4,128]{2,1,0:T(4,128)(2,1)S(1)} %get-tuple-element.2), channel_id=1, source_target_pairs={{0,1},{1,2},{2,3},{3,4},{4,5},{5,6},{6,7},{7,8},{8,9},{9,10},{10,1... | collective-permute-start | bytes 3080 | tf_op jit(solution)/shard_map/ppermute | solution.py:14
  17.2 0.7 fusion.49
  17.9 0.9 fusion.27
  18.8 15.3 %all-gather = bf16[256,16,4]{1,2,0:T(4,128)(2,1)S(1)} all-gather(bf16[32,16,4]{1,2,0:T(4,128)(2,1)S(1)} %fusion.27), channel_id=2, replica_groups=mesh['net'=8,'strip'=16] {'net'}, dimensions={0}, use_global_device_ids=true | all-gather | bytes 36864 | tf_op jit(solution)/shard_map/all_gather | solution.py:82
  34.2 0.2 copy.91
  34.4 0.2 copy.74
  34.6 0.7 broadcast_maximum_fusion
  35.3 0.1 copy.81
  35.4 0.1 reshape.82
  35.4 0.7 broadcast_maximum_fusion.1
  36.1 0.1 copy.75
  36.2 0.1 reshape.74
  36.3 0.7 compare_select_fusion
  37.0 0.1 copy.70
  37.1 0.1 reshape.66
  37.9 32.7 %all_gather.19 = bf16[512,16,32]{2,1,0:T(8,128)(2,1)} all-gather(bf16[32,16,32]{2,1,0:T(8,128)(2,1)S(1)} %copy.74), channel_id=1, replica_groups=mesh['net'=8,'strip'=16] {'strip'}, dimensions={0}, use_global_device_ids=true | all-gather | bytes 557056 | tf_op jit(solution)/shard_map/all_gather | solution.py:84
  70.7 1.9 fusion.31
  72.6 0.1 copy.84
  72.6 4.4 %copy.86 = bf16[32,16,16,16]{2,1,3,0:T(8,128)(2,1)} copy(bf16[32,16,16,16]{0,3,2,1:T(8,128)(2,1)S(1)} %copy-done.4) | data formatting | bytes 524288 | tf_op args[13]
  77.0 0.1 copy.71
  77.1 3.5 %copy.77 = bf16[24,16,16,16]{3,2,1,0:T(8,128)(2,1)} copy(bf16[24,16,16,16]{0,3,2,1:T(8,128)(2,1)S(1)} %copy-done.5) | data formatting | bytes 393216 | tf_op args[7]
  80.6 0.1 copy.76
  80.6 1.9 fusion.29
  82.5 3.2 %gather_fusion = bf16[384,32,128]{2,1,0:T(8,128)(2,1)S(1)} fusion(bf16[384,32,128]{2,1,0:T(8,128)(2,1)} %all-gather.4.cloned.1.call-done, s32[1024]{0:T(1024)S(1)} %pad_clamp_fusion.2), kind=kCustom, calls=%fused_computation | custom fusion | bytes 6292992 | tf_op jit(solution)/shard_map/gather | solution.py:65
  85.7 8.0 %fusion.6 = f32[24,32,128]{2,1,0:T(8,128)} fusion(bf16[24,16,128,128]{3,2,1,0:T(8,128)(2,1)} %param.17, bf16[24,16,32,128]{3,2,1,0:T(8,128)(2,1)S(1)} %bitcast.57, bf16[24,16]{1,0:T(8,128)(2,1)S(1)} %copy.71), kind=kOutput, calls=%fused_computation.10 | convolution fusion | flops 404226048 | bytes 16122624 | tf_op jit(solution)/shard_map/tkpq,tkrq->trp/dot_general | solution.py:66
  93.7 50.4 %all-gather.6.cloned.1.call-done = bf16[3072,16,32]{2,1,0:T(8,128)(2,1)} async-done(((bf16[24,16,32]{2,1,0:T(8,128)(2,1)}), bf16[3072,16,32]{2,1,0:T(8,128)(2,1)}) %all-gather.6.cloned.1.call-update) | async-done | bytes 3145744 | tf_op jit(solution)/shard_map/all_gather | solution.py:83
  144.1 6.8 %constant_dynamic-update-slice_fusion.1 = bf16[3584,16,32]{2,1,0:T(8,128)(2,1)S(1)} fusion(bf16[3072,16,32]{2,1,0:T(8,128)(2,1)} %all-gather.6.cloned.1.call-done), kind=kLoop, calls=%fused_computation.58 | loop fusion | bytes 15728640
  151.0 0.5 constant_dynamic-update-slice_fusion
  151.5 5.2 %copy-done.1 = bf16[3584,16,32]{2,1,0:T(8,128)(2,1)} copy-done((bf16[3584,16,32]{2,1,0:T(8,128)(2,1)}, bf16[3584,16,32]{2,1,0:T(8,128)(2,1)S(1)}, u32[]{:S(2)}) %copy-start.1) | copy-done | bytes 3670040
  156.7 7.8 %constant_dynamic-slice_fusion = bf16[3584,16,4]{2,1,0:T(8,128)(2,1)} fusion(bf16[3584,16,32]{2,1,0:T(8,128)(2,1)S(1)} %constant_dynamic-update-slice_fusion, s32[]{:T(128)S(6)} %select_n.9), kind=kLoop, calls=%fused_computation.62 | loop fusion | bytes 917508 | tf_op jit(solution)/shard_map/dynamic_slice | solution.py:87
  164.5 24.0 %copy.82 = bf16[3584,16,4]{1,2,0:T(4,128)(2,1)} copy(bf16[3584,16,4]{2,1,0:T(8,128)(2,1)} %constant_dynamic-slice_fusion) | data formatting | bytes 917504 | tf_op jit(solution)/shard_map/dynamic_slice | solution.py:87
  188.6 3.5 %gather_fusion.2 = bf16[512,16,4]{1,2,0:T(4,128)(2,1)S(1)} fusion(bf16[3584,16,4]{1,2,0:T(4,128)(2,1)} %copy.82, s32[1024]{0:T(1024)S(1)} %pad_clamp_fusion), kind=kCustom, calls=%fused_computation.2 | custom fusion | bytes 133120 | tf_op jit(solution)/shard_map/gather | solution.py:30
  192.1 0.9 copy.92
  193.0 7.2 %gather_fusion.1 = bf16[384,16,32]{2,1,0:T(8,128)(2,1)} fusion(bf16[3584,16,32]{2,1,0:T(8,128)(2,1)} %copy-done.1, s32[1024]{0:T(1024)S(1)} %pad_clamp_fusion.1), kind=kCustom, calls=%fused_computation.1 | custom fusion | bytes 787968 | tf_op jit(solution)/shard_map/gather | solution.py:30
  200.3 3.9 %fusion.9 = bf16[24,32,128]{2,1,0:T(8,128)(2,1)} fusion(f32[24,32,128]{2,1,0:T(8,128)S(1)} %copy-done.6, bf16[24,16,128]{2,1,0:T(8,128)(2,1)S(1)} %copy-done.8, bf16[24,16,16,16]{3,2,1,0:T(8,128)(2,1)} %copy.77, bf16[24,16,16,32]{3,2,1,0:T(8,128)(2,1)} %bitcast.58, bf16[24,16]{1,0:T(8,128)(2,1)S(1)} %copy.76, f32[24]{0:T(128)S(1)} %compare_convert_fusion.3, ...), kind=kOutput, calls=%fused_computation.11 | convolution fusion | flops 10543104 | bytes 1280352 | tf_op jit(solution)/shard_map/tap,tar->trp/dot_general | solution.py:38
  204.2 0.9 fusion.28
  205.1 2.5 %fusion.25 = bf16[32,4,128]{2,1,0:T(4,128)(2,1)} fusion(f32[32,4,128]{2,1,0:T(4,128)S(1)} %fusion.28, f32[32,4,128]{2,1,0:T(4,128)S(1)} %fusion.29, f32[32,4,128]{2,1,0:T(4,128)S(1)} %fusion.31, bf16[32,3,128,128]{3,2,1,0:T(8,128)(2,1)} %param.23, bf16[32,4,128]{2,1,0:T(4,128)(2,1)S(1)} %copy-done.7, bf16[1,4,128]{2,1,0:T(4,128)(2,1)S(1)} %collective-permute-done), kind=kOutput, calls=%fused_computation.23 | convolution fusion | flops 4327424 | bytes 1311744 | tf_op jit(solution)/shard_map/tpq,trq->trp/dot_general | solution.py:68
  (31 shorter events, 0.1 us)
Async XLA Ops:
  7.2 10.7 %copy-start = (bf16[32,16,128]{2,1,0:T(8,128)(2,1)S(1)}, bf16[32,16,128]{2,1,0:T(8,128)(2,1)}, u32[]{:S(2)}) copy-start(bf16[32,16,128]{2,1,0:T(8,128)(2,1)} %param.24) | copy-start | bytes 393220
  7.2 63.5 %copy-start.7 = (bf16[32,4,128]{2,1,0:T(4,128)(2,1)S(1)}, bf16[32,4,128]{2,1,0:T(4,128)(2,1)}, u32[]{:S(2)}) copy-start(bf16[32,4,128]{2,1,0:T(4,128)(2,1)} %param.22) | copy-start | bytes 98308
  7.2 63.4 %copy-start.9 = (s32[32,16]{0,1:T(8,128)S(1)}, s32[32,16]{0,1:T(8,128)}, u32[]{:S(2)}) copy-start(s32[32,16]{0,1:T(8,128)} %param.26) | copy-start | bytes 6148
  7.2 63.5 %copy-start.11 = (s32[24,16]{0,1:T(8,128)S(1)}, s32[24,16]{0,1:T(8,128)}, u32[]{:S(2)}) copy-start(s32[24,16]{0,1:T(8,128)} %param.20) | copy-start | bytes 4612
  7.2 63.4 %copy-start.10 = (s32[24,16]{0,1:T(8,128)S(1)}, s32[24,16]{0,1:T(8,128)}, u32[]{:S(2)}) copy-start(s32[24,16]{0,1:T(8,128)} %param.16) | copy-start | bytes 4612
  7.2 65.4 %copy-start.4 = (bf16[32,16,16,16]{0,3,2,1:T(8,128)(2,1)S(1)}, bf16[32,16,16,16]{0,3,2,1:T(8,128)(2,1)}, u32[]{:S(2)}) copy-start(bf16[32,16,16,16]{0,3,2,1:T(8,128)(2,1)} %param.27) | copy-start | bytes 786436
  7.2 75.3 %all-gather.4.cloned.1.call-start = ((), (), s32[]{:S(2)}) async-start(), calls=%async_computation | async-start | bytes 3342336 | tf_op jit(solution)/shard_map/all_gather | solution.py:62
  8.0 136.2 %all-gather.6.cloned.1.call-start = ((), (), s32[]{:S(2)}) async-start(), calls=%async_computation.1 | async-start | bytes 12681216 | tf_op jit(solution)/shard_map/all_gather | solution.py:83
  11.3 69.3 %collective-permute-start.1 = (bf16[1,4,128]{2,1,0:T(4,128)(2,1)S(1)}, bf16[1,4,128]{2,1,0:T(4,128)(2,1)S(1)}, u32[]{:S(2)}, u32[]{:S(2)}) collective-permute-start(bf16[1,4,128]{2,1,0:T(4,128)(2,1)S(1)} %get-tuple-element.3), channel_id=1, source_target_pairs={{1,0},{2,1},{3,2},{4,3},{5,4},{6,5},{7,6},{8,7},{9,8},{10,9},{11,1... | collective-permute-start | bytes 3080 | tf_op jit(solution)/shard_map/ppermute | solution.py:15
  12.6 192.5 %collective-permute-start = (bf16[1,4,128]{2,1,0:T(4,128)(2,1)S(1)}, bf16[1,4,128]{2,1,0:T(4,128)(2,1)S(1)}, u32[]{:S(2)}, u32[]{:S(2)}) collective-permute-start(bf16[1,4,128]{2,1,0:T(4,128)(2,1)S(1)} %get-tuple-element.2), channel_id=1, source_target_pairs={{0,1},{1,2},{2,3},{3,4},{4,5},{5,6},{6,7},{7,8},{8,9},{9,10},{10,1... | collective-permute-start | bytes 3080 | tf_op jit(solution)/shard_map/ppermute | solution.py:14
  37.9 39.2 %copy-start.5 = (bf16[24,16,16,16]{0,3,2,1:T(8,128)(2,1)S(1)}, bf16[24,16,16,16]{0,3,2,1:T(8,128)(2,1)}, u32[]{:S(2)}) copy-start(bf16[24,16,16,16]{0,3,2,1:T(8,128)(2,1)} %param.21) | copy-start | bytes 589828
  93.7 57.2 %copy-start.2 = (bf16[512,16,32]{2,1,0:T(8,128)(2,1)S(1)}, bf16[512,16,32]{2,1,0:T(8,128)(2,1)}, u32[]{:S(2)}) copy-start(bf16[512,16,32]{2,1,0:T(8,128)(2,1)} %all_gather.19) | copy-start | bytes 1572868
  151.5 5.2 %copy-start.1 = (bf16[3584,16,32]{2,1,0:T(8,128)(2,1)}, bf16[3584,16,32]{2,1,0:T(8,128)(2,1)S(1)}, u32[]{:S(2)}) copy-start(bf16[3584,16,32]{2,1,0:T(8,128)(2,1)S(1)} %constant_dynamic-update-slice_fusion) | copy-start | bytes 11010052
  192.1 8.2 %copy-start.6 = (f32[24,32,128]{2,1,0:T(8,128)S(1)}, f32[24,32,128]{2,1,0:T(8,128)}, u32[]{:S(2)}) copy-start(f32[24,32,128]{2,1,0:T(8,128)} %fusion.6) | copy-start | bytes 1179652
  192.1 8.2 %copy-start.8 = (bf16[24,16,128]{2,1,0:T(8,128)(2,1)S(1)}, bf16[24,16,128]{2,1,0:T(8,128)(2,1)}, u32[]{:S(2)}) copy-start(bf16[24,16,128]{2,1,0:T(8,128)(2,1)} %param.18) | copy-start | bytes 294916
  200.3 4.0 %copy-start.3 = (bf16[32,16,16,16]{2,1,3,0:T(8,128)(2,1)S(1)}, bf16[32,16,16,16]{2,1,3,0:T(8,128)(2,1)}, u32[]{:S(2)}) copy-start(bf16[32,16,16,16]{2,1,3,0:T(8,128)(2,1)} %copy.86) | copy-start | bytes 786436
Sparse Core Ops, SparseCore 0:
  10.2 54.0 all-gather.3
  67.9 76.2 all-gather.5
